TPU v7x, 512 devices: a whole 4x4x16 slice. The times are simulated.
512 devices in a mesh: row: 16 (over z), col: 8 (over x, core), rep: 4 (over y).
Axes of the slice: x: 4, y: 4, z: 16, core: 2. Of those that a mesh axis runs over, the one named last changes fastest.
Arguments:
- density: float32 [4096, 4096], P(('col', 'rep'), 'row'), may hold values from -0.25 to 1.25, as said below
- pattern: int32 [64, 9], replicated, may hold values from 0 to 63, as said below
- grid_order: int32 [64], replicated, may hold values from 0 to 63, as said below
Outputs:
- purified: float32 [4096, 4096], P(('col', 'rep'), 'row')
Inputs may be any that keep to these rules, and one draw needn't show every extreme that they name: `pattern`: row r lists (r + d) mod 64 for one set of 9 distinct offsets d that holds 0 and is closed under negation modulo 64. `grid_order`: each block index appears once. `density`: Symmetric; zero outside the blocks that the pattern lists.
All inputs are finite; a program needn't handle non-finite values.
Results may differ from a plain program's by a relative error of at most 0.00016.
Values sent between devices are 32-bit elements; how exact they have to be, the bound alone decides.
A program may use at most 64 MiB of HBM per device.

v0:
```python
import jax
import jax.numpy as jnp
from jax import lax
from jax.sharding import PartitionSpec as P

BLOCK = 64
STEPS = 2


def block_mask(pattern, grid_order, first_row, first_col, row_blocks, col_blocks):
    total = grid_order.shape[0]
    every = jnp.arange(total, dtype=jnp.int32)
    row_ids = first_row + jnp.arange(row_blocks, dtype=jnp.int32)
    col_ids = first_col + jnp.arange(col_blocks, dtype=jnp.int32)
    row_pick = (row_ids[:, None] == every[None, :]).astype(jnp.int32)
    col_pick = (col_ids[:, None] == every[None, :]).astype(jnp.int32)
    natural_rows = jnp.sum(row_pick * grid_order[None, :], axis=1)
    natural_cols = jnp.sum(col_pick * grid_order[None, :], axis=1)
    row_select = (natural_rows[:, None] == every[None, :]).astype(jnp.int32)
    listed = jnp.sum(row_select[:, :, None] * pattern[None, :, :], axis=1)
    hits = jnp.any(listed[:, :, None] == natural_cols[None, None, :], axis=1)
    return hits.astype(jnp.float32)


def fold_product(left, panel):
    return jnp.dot(
        lax.all_gather(left, "row", axis=1, tiled=True),
        panel,
        precision=lax.Precision.HIGHEST,
        preferred_element_type=jnp.float32,
    )


def local(density, pattern, grid_order):
    row_count, col_count = density.shape
    row_blocks = row_count // BLOCK
    col_blocks = col_count // BLOCK
    first_row = lax.axis_index(("col", "rep")) * row_blocks
    first_col = lax.axis_index("row") * col_blocks
    hits = block_mask(pattern, grid_order, first_row, first_col, row_blocks, col_blocks)
    mask = jnp.broadcast_to(hits[:, None, :, None], (row_blocks, BLOCK, col_blocks, BLOCK)).reshape(
        row_count, col_count
    )
    current = density
    for repeat in range(STEPS):
        panel = lax.all_gather(current, ("col", "rep"), axis=0, tiled=True)
        square = fold_product(current, panel)
        cube = fold_product(square, panel)
        current = mask * (3.0 * square - 2.0 * cube)
    return current


def solution(mesh):
    in_specs = (P(("col", "rep"), "row"), P(), P())
    out_specs = P(("col", "rep"), "row")
    return jax.shard_map(local, mesh=mesh, in_specs=in_specs, out_specs=out_specs, check_vma=False)
```

profile of v0, /device:TPU:1, one launch (start us, length us, event | category | flops | bytes accessed | tf_op | source)
XLA Modules:
  0.0 444.2 jit_solution(9796100279095620966)
XLA Ops:
  6.5 0.0 all-gather.7.cloned.1.call-start
  6.5 0.7 all-gather.7.cloned.1.call-update
  7.3 0.0 all-gather.9.cloned.1.call-start
  7.3 0.7 all-gather.9.cloned.1.call-update
  8.0 0.0 copy-start.1
  8.0 0.0 copy-start
  8.0 0.0 all-gather.11.cloned.1.call-start
  8.1 70.2 %all-gather.7.cloned.1.call-done = f32[128,4096]{1,0:T(8,128)} async-done(((f32[128,256]{1,0:T(8,128)}), f32[128,4096]{1,0:T(8,128)}) %all-gather.7.cloned.1.call-update) | async-done | bytes 2097168 | tf_op jit(solution)/shard_map/all_gather | solution.py:27
  78.3 70.8 %all-gather.9.cloned.1.call-done = f32[4096,256]{1,0:T(8,128)} async-done(((f32[128,256]{1,0:T(8,128)}), f32[4096,256]{1,0:T(8,128)}) %all-gather.9.cloned.1.call-update) | async-done | bytes 4194320 | tf_op jit(solution)/shard_map/all_gather | solution.py:46
  149.1 5.6 %fusion.5 = f32[128,256]{1,0:T(8,128)} fusion(f32[128,4096]{1,0:T(8,128)} %all-gather.7.cloned.1.call-done, f32[4096,256]{1,0:T(8,128)} %all-gather.9.cloned.1.call-done), kind=kOutput, calls=%fused_computation.15 | convolution fusion | flops 1610612736 | bytes 6422528 | tf_op jit(solution)/shard_map/dot_general | solution.py:26
  154.6 0.0 all-gather.11.cloned.1.call-update
  154.7 0.0 all-gather.13.cloned.1.call-start
  154.7 0.2 fusion.4
  154.9 0.1 compare_convert_fusion
  155.0 0.2 multiply_reduce_fusion
  155.2 0.1 copy.5
  155.3 0.2 select_reduce_fusion
  155.5 0.2 compare_reduce_fusion
  155.7 0.1 broadcast_in_dim.2
  155.8 0.2 reshape.40
  156.0 61.4 %all-gather.11.cloned.1.call-done = f32[128,4096]{1,0:T(8,128)} async-done(((f32[128,256]{1,0:T(8,128)}), f32[128,4096]{1,0:T(8,128)}) %all-gather.11.cloned.1.call-update) | async-done | bytes 2097168 | tf_op jit(solution)/shard_map/all_gather | solution.py:27
  217.4 5.6 %fusion.3 = f32[128,256]{1,0:T(8,128)} fusion(f32[128,256]{1,0:T(8,128)S(1)} %reshape.40, f32[128,4096]{1,0:T(8,128)} %all-gather.11.cloned.1.call-done, f32[4096,256]{1,0:T(8,128)} %all-gather.9.cloned.1.call-done, f32[128,256]{1,0:T(8,128)} %fusion.5), kind=kOutput, calls=%fused_computation.5 | convolution fusion | flops 1610743808 | bytes 6684672 | tf_op jit(solution)/shard_map/dot_general | solution.py:26
  223.1 0.0 all-gather.13.cloned.1.call-update
  223.1 0.0 all-gather.15.cloned.1.call-start
  223.1 0.5 all-gather.15.cloned.1.call-update
  223.7 0.0 all-gather.17.cloned.1.call-start
  223.7 68.9 %all-gather.13.cloned.1.call-done = f32[128,4096]{1,0:T(8,128)} async-done(((f32[128,256]{1,0:T(8,128)}), f32[128,4096]{1,0:T(8,128)}) %all-gather.13.cloned.1.call-update) | async-done | bytes 2097168 | tf_op jit(solution)/shard_map/all_gather | solution.py:27
  292.7 70.6 %all-gather.15.cloned.1.call-done = f32[4096,256]{1,0:T(8,128)} async-done(((f32[128,256]{1,0:T(8,128)}), f32[4096,256]{1,0:T(8,128)}) %all-gather.15.cloned.1.call-update) | async-done | bytes 4194320 | tf_op jit(solution)/shard_map/all_gather | solution.py:46
  363.3 5.6 %fusion.6 = f32[128,256]{1,0:T(8,128)} fusion(f32[128,4096]{1,0:T(8,128)} %all-gather.13.cloned.1.call-done, f32[4096,256]{1,0:T(8,128)} %all-gather.15.cloned.1.call-done), kind=kOutput, calls=%fused_computation.16 | convolution fusion | flops 1610612736 | bytes 6422528 | tf_op jit(solution)/shard_map/dot_general | solution.py:26
  368.9 0.0 all-gather.17.cloned.1.call-update
  368.9 62.8 %all-gather.17.cloned.1.call-done = f32[128,4096]{1,0:T(8,128)} async-done(((f32[128,256]{1,0:T(8,128)}), f32[128,4096]{1,0:T(8,128)}) %all-gather.17.cloned.1.call-update) | async-done | bytes 2097168 | tf_op jit(solution)/shard_map/all_gather | solution.py:27
  431.7 5.6 %fusion.1 = f32[128,256]{1,0:T(8,128)} fusion(f32[128,256]{1,0:T(8,128)S(1)} %reshape.40, f32[128,4096]{1,0:T(8,128)} %all-gather.17.cloned.1.call-done, f32[4096,256]{1,0:T(8,128)} %all-gather.15.cloned.1.call-done, f32[128,256]{1,0:T(8,128)} %fusion.6), kind=kOutput, calls=%fused_computation.2 | convolution fusion | flops 1610743808 | bytes 6684672 | tf_op jit(solution)/shard_map/dot_general | solution.py:26
  (5 shorter events, 0.0 us)
Async XLA Ops:
  6.5 71.7 %all-gather.7.cloned.1.call-start = ((), (), s32[]{:S(2)}) async-start(), calls=%async_computation | async-start | bytes 2228224 | tf_op jit(solution)/shard_map/all_gather | solution.py:27
  7.3 141.8 %all-gather.9.cloned.1.call-start = ((), (), s32[]{:S(2)}) async-start(), calls=%async_computation.1 | async-start | bytes 4325376 | tf_op jit(solution)/shard_map/all_gather | solution.py:46
  8.0 146.7 %copy-start.1 = (s32[64]{0:T(128)S(1)}, s32[64]{0:T(128)}, u32[]{:S(2)}) copy-start(s32[64]{0:T(128)} %param.5) | copy-start | bytes 772
  8.0 147.0 %copy-start = (s32[64,9]{0,1:T(8,128)S(1)}, s32[64,9]{0,1:T(8,128)}, u32[]{:S(2)}) copy-start(s32[64,9]{0,1:T(8,128)} %param.4) | copy-start | bytes 6916
  8.0 209.4 %all-gather.11.cloned.1.call-start = ((), (), s32[]{:S(2)}) async-start(), calls=%async_computation.2 | async-start | bytes 2228224 | tf_op jit(solution)/shard_map/all_gather | solution.py:27
  154.7 138.0 %all-gather.13.cloned.1.call-start = ((), (), s32[]{:S(2)}) async-start(), calls=%async_computation.3 | async-start | bytes 2228224 | tf_op jit(solution)/shard_map/all_gather | solution.py:27
  223.1 140.2 %all-gather.15.cloned.1.call-start = ((), (), s32[]{:S(2)}) async-start(), calls=%async_computation.4 | async-start | bytes 4325376 | tf_op jit(solution)/shard_map/all_gather | solution.py:46
  223.7 208.0 %all-gather.17.cloned.1.call-start = ((), (), s32[]{:S(2)}) async-start(), calls=%async_computation.5 | async-start | bytes 2228224 | tf_op jit(solution)/shard_map/all_gather | solution.py:27
Sparse Core Ops, SparseCore 0:
  9.4 68.8 all-gather.6
  81.4 67.6 all-gather.8
  154.8 62.6 all-gather.10
  223.2 69.4 all-gather.12
  295.7 67.6 all-gather.14
  369.0 62.6 all-gather.16
where the time goes:
time: 452 us; the launch traced here: 444 us
  waiting for transfers between devices  407 us (90%)
  matrix products  22.4 us (5%)
  between operations  13.5 us (3%)
    all_gather x4, waiting for transfers between devices, fold_product(): lax.all_gather(left, 'row', axis=1, tiled=True)  263 us
    all_gather x2, waiting for transfers between devices, local(): panel = lax.all_gather(current, ('col', 'rep'), axis=0, tiled=True)  141 us
    dot_general x4, matrix products, fold_product(): jnp.dot(lax.all_gather(left, 'row', axis=1, tiled=True), panel, precision...  22.4 us
  transfers between devices with their start and end apart: 6, of which 6 were waited for; matrix products, arithmetic and copies ran while one was open for 0% of the time, Pallas kernels for 0%

commit v1 on v0

v1 whole, which is shorter than its diff:
```python
import jax
import jax.numpy as jnp
from jax import lax
from jax.experimental import pallas as pl
from jax.experimental.pallas import tpu as pltpu
from jax.sharding import PartitionSpec as P

MESH = pl.DeviceIdType.MESH
F32 = jnp.float32
PLANES = 16
DEVS = 32
NB = 64
ROWS = 9
PAIRS = 5
LANES = 128
HI = lax.Precision.HIGHEST
CHUNK = (PAIRS, 8, LANES)
BATCHES = [(0, 1)] + [(2 * b - 1, 2) for b in range(1, 8)] + [(15, 1)]


class Place:
    def __init__(self):
        self.r = lax.axis_index("row")
        self.c = lax.axis_index("col")
        self.p = lax.axis_index("rep")
        self.me = self.c * 4 + self.p
        self.jj = self.c % 4
        self.core = self.c % 2
        self.s = (self.c // 4) * 4 + self.p
        partner_c = self.c + 2 - 4 * ((self.c // 2) % 2)
        sibling_c = self.c + 1 - 2 * self.core
        self.jp = partner_c % 4
        self.js = sibling_c % 4
        self.jq = (partner_c + 1 - 2 * self.core) % 4
        self.partner = (self.r, partner_c, self.p)
        self.sibling = (self.r, sibling_c, self.p)

    def plane(self, d):
        return (self.r, d // 4, d % 4)

    def along(self, d):
        return (lax.rem(self.r + d + PLANES, PLANES), self.c, self.p)

    def slice_owner(self, s2):
        return (self.r, (s2 // 4) * 4 + self.jj, s2 % 4)

    def chip(self, t):
        d = lax.rem((self.c // 2) * 4 + self.p + t, 16)
        return d, (self.r, (d // 4) * 2 + self.core, d % 4)


def put(src, dst, ssem, rsem, dev):
    pltpu.make_async_remote_copy(
        src_ref=src, dst_ref=dst, send_sem=ssem, recv_sem=rsem, device_id=dev, device_id_type=MESH
    ).start()


def take(ref, sem):
    pltpu.make_async_copy(ref, ref, sem).wait()


def signal(dev):
    pl.semaphore_signal(pltpu.get_barrier_semaphore(), inc=1, device_id=dev, device_id_type=MESH)


def times(first, last, body):
    def step(t, carry):
        body(t)
        return carry

    lax.fori_loop(first, last, step, 0)


def scatter_kernel(dens, landed, send, recv):
    at = Place()
    times(1, DEVS, lambda t: signal(at.plane(lax.rem(at.me + t, DEVS))))
    pl.semaphore_wait(pltpu.get_barrier_semaphore(), DEVS - 1)

    def lanes(c):
        return pl.ds(pl.multiple_of(((c % 4) // 2) * LANES, LANES), LANES)

    mine = landed.at[pl.ds(2 * at.me, 2)]

    def one(t):
        d = lax.rem(at.me + t, DEVS)
        dc = d // 4
        put(dens.at[:, (dc // 4) * 4 + d % 4, :, lanes(dc)], mine, send, recv, at.plane(d))

    times(1, DEVS, one)
    landed[pl.ds(2 * at.me, 2)] = dens[:, at.s, :, lanes(at.c)]
    rest = landed.at[pl.ds(0, 2 * (DEVS - 1))]
    take(rest, recv)
    take(rest, send)


def column_reduce(at, ct, rs, send, recv):
    def one(u):
        s2 = lax.rem(at.s + u, 8)
        put(ct.at[s2], rs.at[at.s], send, recv, at.slice_owner(s2))

    times(1, 8, one)
    rs[at.s] = ct[at.s]
    take(rs.at[pl.ds(0, 7)], recv)


def updated(sq, rs, t):
    acc = rs[0, t]
    for k in range(1, 8):
        acc = acc + rs[k, t]
    return 3.0 * sq[t] - 2.0 * acc


def meet_neighbours(at):
    for d in (1, -1, 2, -2):
        signal(at.along(d))
    times(1, 8, lambda u: signal(at.slice_owner(lax.rem(at.s + u, 8))))
    signal(at.partner)
    signal(at.sibling)
    pl.semaphore_wait(pltpu.get_barrier_semaphore(), 13)


def spread(at, own, x, bbuf, z_send, z_recv, par_send, par_recv, sib_send, sib_recv, b_send, b_recv):
    mine = x.at[at.jj]
    for d, o in ((1, 1), (-1, 2), (2, 3), (-2, 4)):
        put(own, mine.at[o], z_send, z_recv.at[o], at.along(d))

    def column(u):
        put(own, bbuf.at[at.s], b_send, b_recv, at.slice_owner(lax.rem(at.s + u, 8)))

    times(1, 8, column)
    put(own, mine.at[0], par_send, par_recv.at[0], at.partner)
    put(own, mine.at[0], sib_send.at[0], sib_recv.at[0], at.sibling)
    x[at.jj, 0] = own[...]
    bbuf[at.s] = own[...]

    def relay(b):
        part = x.at[at.jp, pl.ds(*BATCHES[b])]
        take(part, par_recv.at[b])
        put(part, part, sib_send.at[1], sib_recv.at[1], at.sibling)

    for b in range(1, 9):
        first, n = BATCHES[b]
        for o in range(first, first + n):
            take(mine.at[o], z_recv.at[o])
            if o + 4 <= 15:
                put(mine.at[o], mine.at[o + 4], z_send, z_recv.at[o + 4], at.along(2 if o % 2 == 1 else -2))
        part = mine.at[pl.ds(first, n)]
        put(part, part, par_send, par_recv.at[b], at.partner)
        put(part, part, sib_send.at[0], sib_recv.at[0], at.sibling)
        if b >= 3:
            relay(b - 3)
    for b in range(6, 9):
        relay(b)
    take(bbuf.at[pl.ds(0, 7)], b_recv)
    take(x.at[at.js], sib_recv.at[0])
    take(x.at[at.jq], sib_recv.at[1])
    take(mine.at[pl.ds(0, 15)], z_send)
    take(mine, par_send)
    take(mine, sib_send.at[0])
    take(mine, sib_send.at[1])
    take(bbuf.at[pl.ds(0, 7)], b_send)


def first_spread_kernel(own, x, bbuf, *sems):
    at = Place()
    meet_neighbours(at)
    spread(at, own, x, bbuf, *sems)


def next_spread_kernel(ct, sq, x, bbuf, rs, own, rs_send, rs_recv, *sems):
    at = Place()
    meet_neighbours(at)
    column_reduce(at, ct, rs, rs_send, rs_recv)
    for t in range(PAIRS):
        own[t] = updated(sq, rs, t)
    spread(at, own, x, bbuf, *sems)
    take(rs.at[pl.ds(0, 7)], rs_send)


def gather_kernel(ct, sq, full, rs, own, rs_send, rs_recv, send, recv, sib_send, sib_recv):
    at = Place()
    times(1, 16, lambda t: signal(at.chip(t)[1]))
    signal(at.sibling)
    pl.semaphore_wait(pltpu.get_barrier_semaphore(), 16)
    column_reduce(at, ct, rs, rs_send, rs_recv)
    for t in range(PAIRS):
        own[t] = updated(sq, rs, t)
    slot = at.core * 16 + (at.c // 2) * 4 + at.p

    def one(t):
        put(own, full.at[slot], send, recv.at[t], at.chip(t)[1])

    times(1, 16, one)
    put(own, full.at[slot], sib_send, sib_recv, at.sibling)
    full[slot] = own[...]

    def forward(t):
        d = lax.rem((at.c // 2) * 4 + at.p + 16 - t, 16)
        part = full.at[at.core * 16 + d]
        take(part, recv.at[t])
        put(part, part, sib_send, sib_recv, at.sibling)

    times(1, 16, forward)
    theirs = full.at[pl.ds((1 - at.core) * 16, 16)]
    take(theirs, sib_recv)
    take(theirs, sib_send)
    take(full.at[pl.ds(0, 15)], send)
    take(rs.at[pl.ds(0, 7)], rs_send)


def low_half():
    return lax.broadcasted_iota(jnp.int32, (8, LANES), 1) < 64


def turn(v):
    return pltpu.roll(v, 64, 1)


def compact_kernel(landed, pat, order, own, inv, pos, place):
    at = Place()
    low = low_half()

    def clear(o):
        inv[o] = jnp.int32(ROWS)

    times(0, NB, clear)

    def locate(q):
        place[order[q]] = q

    times(0, NB, locate)
    nj = order[4 * at.r + at.jj]
    for a in range(ROWS):
        off = pat[0, a]
        inv[off] = jnp.int32(a)
        pos[a] = place[(nj + off) & (NB - 1)]
    for t in range(PAIRS):
        v0 = landed[pos[2 * t]]
        lo = jnp.where(at.core == 0, v0, turn(v0))
        if 2 * t + 1 < ROWS:
            v1 = landed[pos[2 * t + 1]]
            hi = jnp.where(at.core == 1, v1, turn(v1))
        else:
            hi = jnp.zeros_like(v0)
        own[t] = jnp.where(low, lo, hi)


def product_kernel(x, bbuf, pat, inv, pos, ct, sq, xa, g, bm, tt):
    at = Place()
    low = low_half()
    zero = jnp.zeros((8, LANES), F32)
    offs = [pat[0, a] for a in range(ROWS)]
    for t in range(PAIRS):
        for k in range(8):
            v = bbuf[k, t]
            bm[128 * t + 8 * k:128 * t + 8 * k + 8] = v[:, :64]
            bm[128 * t + 64 + 8 * k:128 * t + 72 + 8 * k] = v[:, 64:]
    for a in range(ROWS):
        i = pos[a]
        ahead = (at.r - (i >> 2)) & (PLANES - 1)
        o = jnp.where(ahead == 0, 0, jnp.where(ahead <= 8, 2 * ahead - 1, 2 * (PLANES - ahead)))
        keep = low if a % 2 == 0 else jnp.logical_not(low)
        for t in range(PAIRS):
            v = x[i & 3, o, t]
            for h in range(2):
                xa[a * 10 + 2 * t + h] = jnp.where(keep, v if h == a % 2 else turn(v), zero)

    def rows_of(k):
        row = pl.multiple_of(8 * k, 8)
        for t in range(PAIRS):
            v = xa[20 * t + inv[(k - offs[2 * t]) & (NB - 1)]]
            if 2 * t + 1 < ROWS:
                v = v + xa[20 * t + 10 + inv[(k - offs[2 * t + 1]) & (NB - 1)]]
            g[pl.ds(row, 8), t * LANES:(t + 1) * LANES] = v

    times(0, NB, rows_of)
    tmat = jnp.dot(g[...], bm[...], precision=HI, preferred_element_type=F32)
    tt[...] = jnp.concatenate([tmat, tmat], axis=1)
    cube = jnp.dot(tmat.T, g[...], precision=HI, preferred_element_type=F32)
    for t in range(PAIRS):
        w = cube[:, t * LANES:(t + 1) * LANES].T
        w = jnp.concatenate([w[:64], w[64:]], axis=1)
        for k in range(8):
            ct[k, t] = w[8 * k:8 * k + 8]
        sq0 = tt[pl.ds(pl.multiple_of(8 * offs[2 * t], 8), 8)]
        sq1 = zero
        if 2 * t + 1 < ROWS:
            sq1 = tt[pl.ds(pl.multiple_of(8 * offs[2 * t + 1], 8), 8)]
        sq[t] = jnp.where(low, sq0, sq1)


def tile_kernel(full, order, inv, out):
    at = Place()
    low = low_half()
    for b in range(2):
        ni = order[2 * at.me + b]
        for hp in range(2):
            find = [inv[(ni - order[4 * at.r + 2 * hp + q]) & (NB - 1)] for q in range(2)]
            for k in range(8):
                got = []
                for q in range(2):
                    v = full[16 * q + (2 * (k // 4) + hp) * 4 + k % 4, find[q] >> 1]
                    got.append(jnp.where((find[q] & 1) == q, v, turn(v)))
                out[b, k, :, hp * LANES:(hp + 1) * LANES] = jnp.where(low, got[0], got[1])


VM = pl.BlockSpec(memory_space=pltpu.VMEM)
SM = pl.BlockSpec(memory_space=pltpu.SMEM)
DMA = pltpu.SemaphoreType.DMA
SPREAD_SEMS = [DMA, DMA((PLANES,)), DMA, DMA((9,)), DMA((2,)), DMA((2,)), DMA, DMA]


def shape(*dims):
    return jax.ShapeDtypeStruct(dims, F32)


def call(body, ident, in_specs, out_shape, scratch, out_specs=None):
    extra = {} if ident is None else {"collective_id": ident, "has_side_effects": True}
    return pl.pallas_call(
        body,
        out_shape=out_shape,
        in_specs=in_specs,
        out_specs=out_specs or jax.tree.map(lambda _: VM, out_shape),
        scratch_shapes=scratch,
        compiler_params=pltpu.CompilerParams(**extra),
    )


def local(density, pattern, grid_order):
    landed = call(scatter_kernel, 0, [VM], shape(NB, 8, LANES), [DMA, DMA])(density.reshape(2, 8, 8, 256))
    own, inv, pos = call(
        compact_kernel, None, [VM, SM, SM],
        (shape(*CHUNK), jax.ShapeDtypeStruct((NB,), jnp.int32), jax.ShapeDtypeStruct((ROWS,), jnp.int32)),
        [pltpu.SMEM((NB,), jnp.int32)], (VM, SM, SM),
    )(landed, pattern, grid_order)
    spread_out = (shape(4, PLANES, *CHUNK), shape(8, *CHUNK))
    x, bbuf = call(first_spread_kernel, 1, [VM], spread_out, SPREAD_SEMS)(own)
    product = call(
        product_kernel, None, [VM, VM, SM, SM, SM], (shape(8, *CHUNK), shape(*CHUNK)),
        [
            pltpu.VMEM((ROWS * 10, 8, LANES), F32),
            pltpu.VMEM((NB * 8, PAIRS * LANES), F32),
            pltpu.VMEM((PAIRS * LANES, 64), F32),
            pltpu.VMEM((NB * 8, LANES), F32),
        ],
    )
    ct, sq = product(x, bbuf, pattern, inv, pos)
    sums = [pltpu.VMEM((8, *CHUNK), F32), pltpu.VMEM(CHUNK, F32), DMA, DMA]
    x, bbuf = call(next_spread_kernel, 2, [VM, VM], spread_out, sums + SPREAD_SEMS)(ct, sq)
    ct, sq = product(x, bbuf, pattern, inv, pos)
    full = call(gather_kernel, 3, [VM, VM], shape(DEVS, *CHUNK), sums + [DMA, DMA((16,)), DMA, DMA])(ct, sq)
    out = call(tile_kernel, None, [VM, SM, SM], shape(2, 8, 8, 256), [])(full, grid_order, inv)
    return out.reshape(128, 256)


def solution(mesh):
    in_specs = (P(("col", "rep"), "row"), P(), P())
    out_specs = P(("col", "rep"), "row")
    return jax.shard_map(local, mesh=mesh, in_specs=in_specs, out_specs=out_specs, check_vma=False)
```

time: 452 us -> 116 us (0.26); the launches traced: 444 us -> 116 us
  waiting for transfers between devices: 407 us -> 0 us
  Pallas kernels: 0 us -> 114 us
  matrix products: 22.4 us -> 0 us
  between operations: 13.5 us -> 0.04 us
    all_gather x6 -> x0, waiting for transfers between devices: 405 us -> none  [the longest x4 263 us: fold_product(): lax.all_gather(left, 'row', axis=1, tiled=True)]
    pallas_call x0 -> x8, Pallas kernels: none -> 114 us  [the longest x1 30.1 us: local(): x, bbuf = call(first_spread_kernel, 1, [VM], spread_out, SPREAD_SEMS)(own)]
    dot_general x4 -> x0, matrix products: 22.4 us -> none  [fold_product(): jnp.dot(lax.all_gather(left, 'row', axis=1, tiled=True), panel, precision...]
  transfers between devices with their start and end apart: 6 -> 0, of which waited for: 6 -> 0; matrix products, arithmetic and copies ran while one was open for 0% -> 0% of each run, Pallas kernels for 0% -> 0%
where the time goes in v1:
time: 116 us
  Pallas kernels  114 us (98%)
  local copies, waits for them, and re-layouts  1.4 us (1%)
    pallas_call x1, Pallas kernels, local(): x, bbuf = call(first_spread_kernel, 1, [VM], spread_out, SPREAD_SEMS)(own)  30.1 us
    pallas_call x1, Pallas kernels, local(): call(next_spread_kernel, 2, [VM, VM], spread_out, sums + SPREAD_SEMS)  29.3 us
    pallas_call x1, Pallas kernels, local(): call(gather_kernel, 3, [VM, VM], shape(DEVS, *CHUNK), sums + [DMA, DMA((1...  19.2 us
    pallas_call x1, Pallas kernels, local(): call(scatter_kernel, 0, [VM], shape(NB, 8, LANES), [DMA, DMA])  18 us
    pallas_call x2, Pallas kernels, local(): ct, sq = product(x, bbuf, pattern, inv, pos)  12.5 us
    pallas_call x1, Pallas kernels, local(): call(compact_kernel, None, [VM, SM, SM], (shape(*CHUNK), jax.ShapeDtypeSt...  3.06 us

profile of v1, /device:TPU:1, one launch (start us, length us, event | category | flops | bytes accessed | tf_op | source)
XLA Modules:
  0.0 115.5 jit_solution(9010672170363173624)
XLA Ops:
  0.0 1.4 %copy.4.pat = s32[64,9]{1,0:T(8,128)} copy(s32[64,9]{0,1:T(8,128)} %param.4) | data formatting | bytes 4608 | tf_op args[1]
  1.4 18.0 %shard_map.37.landed = f32[64,8,128]{2,1,0:T(8,128)} custom-call(f32[2,8,8,256]{3,2,1,0:T(8,128)} %bitcast.2), custom_call_target="tpu_custom_call" | custom-call | tf_op jit(solution)/shard_map/pallas_call | solution.py:330
  19.4 3.1 %shard_map.38 = (f32[5,8,128]{2,1,0:T(8,128)}, s32[64]{0:T(128)}, s32[9]{0:T(128)}) custom-call(f32[64,8,128]{2,1,0:T(8,128)} %shard_map.37.landed, s32[64,9]{1,0:T(8,128)} %copy.4.pat, s32[64]{0:T(128)} %order.3), custom_call_target="tpu_custom_call" | custom-call | tf_op jit(solution)/shard_map/pallas_call | solution.py:331
  22.5 30.1 %shard_map.39 = (f32[4,16,5,8,128]{4,3,2,1,0:T(8,128)}, f32[8,5,8,128]{3,2,1,0:T(8,128)}) custom-call(f32[5,8,128]{2,1,0:T(8,128)} %get-tuple-element.16.own), custom_call_target="tpu_custom_call" | custom-call | tf_op jit(solution)/shard_map/pallas_call | solution.py:337
  52.6 6.3 %shard_map.40 = (f32[8,5,8,128]{3,2,1,0:T(8,128)}, f32[5,8,128]{2,1,0:T(8,128)}) custom-call(f32[4,16,5,8,128]{4,3,2,1,0:T(8,128)} %get-tuple-element.17.x, f32[8,5,8,128]{3,2,1,0:T(8,128)} %get-tuple-element.18.bbuf, s32[64,9]{1,0:T(8,128)} %copy.4.pat, s32[64]{0:T(128)} %get-tuple-element.19.inv, s32[9]{0:T(128)} %get-tuple-element.20.pos), custom_call_target="tpu_custom_call" | custom-call | tf_op jit(solution)/shard_map/pallas_call | solution.py:347
  58.8 29.3 %shard_map.41 = (f32[4,16,5,8,128]{4,3,2,1,0:T(8,128)}, f32[8,5,8,128]{3,2,1,0:T(8,128)}) custom-call(f32[8,5,8,128]{3,2,1,0:T(8,128)} %get-tuple-element.21.ct, f32[5,8,128]{2,1,0:T(8,128)} %get-tuple-element.22.sq), custom_call_target="tpu_custom_call" | custom-call | tf_op jit(solution)/shard_map/pallas_call | solution.py:349
  88.2 6.3 %shard_map.42 = (f32[8,5,8,128]{3,2,1,0:T(8,128)}, f32[5,8,128]{2,1,0:T(8,128)}) custom-call(f32[4,16,5,8,128]{4,3,2,1,0:T(8,128)} %get-tuple-element.23.x, f32[8,5,8,128]{3,2,1,0:T(8,128)} %get-tuple-element.24.bbuf, s32[64,9]{1,0:T(8,128)} %copy.4.pat, s32[64]{0:T(128)} %get-tuple-element.19.inv, s32[9]{0:T(128)} %get-tuple-element.20.pos), custom_call_target="tpu_custom_call" | custom-call | tf_op jit(solution)/shard_map/pallas_call | solution.py:350
  94.4 19.2 %shard_map.43.full = f32[32,5,8,128]{3,2,1,0:T(8,128)} custom-call(f32[8,5,8,128]{3,2,1,0:T(8,128)} %get-tuple-element.25.ct, f32[5,8,128]{2,1,0:T(8,128)} %get-tuple-element.26.sq), custom_call_target="tpu_custom_call" | custom-call | tf_op jit(solution)/shard_map/pallas_call | solution.py:351
  113.6 1.9 %shard_map.44 = f32[2,8,8,256]{3,2,1,0:T(8,128)} custom-call(f32[32,5,8,128]{3,2,1,0:T(8,128)} %shard_map.43.full, s32[64]{0:T(128)} %order.3, s32[64]{0:T(128)} %get-tuple-element.19.inv), custom_call_target="tpu_custom_call" | custom-call | tf_op jit(solution)/shard_map/pallas_call | solution.py:352

commit v2 on v0

v2 whole, which is shorter than its diff:
```python
import jax
import jax.numpy as jnp
from jax import lax
from jax.experimental import pallas as pl
from jax.experimental.pallas import tpu as pltpu
from jax.sharding import PartitionSpec as P

MESH = pl.DeviceIdType.MESH
F32 = jnp.float32
BF16 = jnp.bfloat16
PLANES = 16
CHIPS = 16
DEVS = 32
NB = 64
ROWS = 9
PAIRS = 5
LANES = 128
WIDE = PAIRS * LANES
CHUNK = (PAIRS, 8, LANES)
POS = NB
OFF = POS + 2 * ROWS
TABLE = 96

PARENT = {1: 0, 2: 0, 4: 0, 3: 4, 5: 4, 6: 4, 7: 4, 8: 4}
FIRST = (4, 2, 1)
ONWARD = (8, 7, 6, 3, 5)
ARRIVAL = (1, 2, 4, 5, 3, 6, 7, 8)
REACH = {1: 8, -1: 7}
JUMPS = (1, 2, 3, 4)


class Place:
    def __init__(self):
        self.r = lax.axis_index("row")
        self.c = lax.axis_index("col")
        self.p = lax.axis_index("rep")
        self.me = self.c * 4 + self.p
        self.core = self.c % 2
        self.chip = (self.c // 2) * 4 + self.p
        self.sibling = (self.r, self.c + 1 - 2 * self.core, self.p)

    def plane(self, d):
        return (self.r, d // 4, d % 4)

    def along(self, d):
        return (lax.rem(self.r + d + PLANES, PLANES), self.c, self.p)

    def other(self, t):
        d = lax.rem(self.chip + t, CHIPS)
        return d, (self.r, (d // 4) * 2 + self.core, d % 4)


def put(src, dst, ssem, rsem, dev):
    pltpu.make_async_remote_copy(
        src_ref=src, dst_ref=dst, send_sem=ssem, recv_sem=rsem, device_id=dev, device_id_type=MESH
    ).start()


def take(ref, sem):
    pltpu.make_async_copy(ref, ref, sem).wait()


def signal(dev):
    pl.semaphore_signal(pltpu.get_barrier_semaphore(), inc=1, device_id=dev, device_id_type=MESH)


def met(n):
    pl.semaphore_wait(pltpu.get_barrier_semaphore(), n)


def times(first, last, body):
    def step(t, carry):
        body(t)
        return carry

    lax.fori_loop(first, last, step, 0)


def greet_along(at):
    for d in JUMPS:
        signal(at.along(d))
        signal(at.along(-d))


def lane_low():
    return lax.broadcasted_iota(jnp.int32, (8, LANES), 1) < 64


def row_low():
    return lax.broadcasted_iota(jnp.int32, (8, LANES), 0) < 4


def turn(v):
    return pltpu.roll(v, 64, 1)


def flip(v):
    return pltpu.roll(v, 4, 0)


def quadrants(q00, q01, q10, q11):
    low = lane_low()
    return jnp.where(row_low(), jnp.where(low, q00, q01), jnp.where(low, q10, q11))


def spread(at, own, x, bbuf, z_send, z_recv, sib_send, sib_recv, b_send, b_recv):
    mine = x.at[at.core]

    def slot(sign, q):
        return 2 * q - 1 if sign > 0 else 2 * q

    def send(src, sign, q):
        o = slot(sign, q)
        put(src, mine.at[o], z_send, z_recv.at[o], at.along(sign * (q - PARENT[q])))

    for q in FIRST:
        for sign in (1, -1):
            send(own, sign, q)

    def column(t):
        put(own, bbuf.at[at.chip], b_send, b_recv, at.other(t)[1])

    put(own, mine.at[0], sib_send, sib_recv, at.sibling)
    times(1, CHIPS, column)
    x[at.core, 0] = own[...]
    bbuf[at.chip] = own[...]
    for q in ARRIVAL:
        signs = [sign for sign in (1, -1) if q <= REACH[sign]]
        for sign in signs:
            part = mine.at[slot(sign, q)]
            take(part, z_recv.at[slot(sign, q)])
            for k in ONWARD:
                if PARENT[k] == q and k <= REACH[sign]:
                    send(part, sign, k)
        for sign in signs:
            part = mine.at[slot(sign, q)]
            put(part, part, sib_send, sib_recv, at.sibling)
    take(bbuf.at[pl.ds(0, CHIPS - 1)], b_recv)
    take(x.at[1 - at.core], sib_recv)
    take(mine.at[pl.ds(0, PLANES - 1)], z_send)
    take(mine, sib_send)
    take(bbuf.at[pl.ds(0, CHIPS - 1)], b_send)


def first_kernel(dens, tab, x, bbuf, landed, own, p_send, p_recv, *sems):
    at = Place()
    times(1, DEVS, lambda t: signal(at.plane(lax.rem(at.me + t, DEVS))))
    greet_along(at)
    met(DEVS - 1 + 2 * len(JUMPS))

    def lanes(c):
        return pl.ds(pl.multiple_of((c % 2) * LANES, LANES), LANES)

    def one(t):
        d = lax.rem(at.me + t, DEVS)
        dc = d // 4
        tile_row = (dc // 2) * 2 + (d % 4) // 2
        put(dens.at[:, tile_row, :, lanes(dc)], landed.at[pl.ds(2 * at.me, 2)], p_send, p_recv, at.plane(d))

    times(1, DEVS, one)
    landed[pl.ds(2 * at.me, 2)] = dens[:, at.chip // 2, :, lanes(at.c)]
    rest = landed.at[pl.ds(0, 2 * (DEVS - 1))]
    take(rest, p_recv)
    for t in range(PAIRS):
        parts = []
        for q in range(2):
            for h in range(2):
                a = 2 * t + h
                if a == ROWS:
                    parts.append(jnp.zeros((8, LANES), F32))
                    continue
                v = landed[tab[POS + q * ROWS + a]]
                v = v if h == q else turn(v)
                parts.append(jnp.where(at.p % 2 == q, v, flip(v)))
        own[t] = quadrants(*parts)
    spread(at, own, x, bbuf, *sems)
    take(rest, p_send)


def reduce_slices(at, ct, sq, rs, own, send, recv):
    def one(t):
        d, dev = at.other(t)
        put(ct.at[d], rs.at[at.chip], send, recv, dev)

    times(1, CHIPS, one)
    rs[at.chip] = ct[at.chip]
    take(rs.at[pl.ds(0, CHIPS - 1)], recv)
    for t in range(PAIRS):
        acc = rs[0, t]
        for k in range(1, CHIPS):
            acc = acc + rs[k, t]
        own[t] = 3.0 * sq[t] - 2.0 * acc


def next_kernel(ct, sq, x, bbuf, rs, own, rs_send, rs_recv, *sems):
    at = Place()
    times(1, CHIPS, lambda t: signal(at.other(t)[1]))
    signal(at.sibling)
    greet_along(at)
    met(CHIPS + 2 * len(JUMPS))
    reduce_slices(at, ct, sq, rs, own, rs_send, rs_recv)
    spread(at, own, x, bbuf, *sems)
    take(rs.at[pl.ds(0, CHIPS - 1)], rs_send)


def last_kernel(ct, sq, order, tab, out, rs, own, dup, fsend, frecv, rs_send, rs_recv, send, recv):
    at = Place()
    times(1, DEVS, lambda t: signal(at.plane(lax.rem(at.me + t, DEVS))))
    met(DEVS - 1)
    reduce_slices(at, ct, sq, rs, own, rs_send, rs_recv)
    low = lane_low()
    for t in range(PAIRS):
        v = own[t]
        w = turn(v)
        dup[2 * t] = jnp.where(low, v, w)
        dup[2 * t + 1] = jnp.where(low, w, v)
    n0 = order[4 * at.r + 2 * at.core]
    n1 = order[4 * at.r + 2 * at.core + 1]

    def dense(d):
        parts = [dup[tab[(order[2 * d + b] - n) & (NB - 1)]] for n in (n0, n1) for b in range(2)]
        fsend[d] = quadrants(*parts)

    times(0, DEVS, dense)

    def give(t):
        d = lax.rem(at.me + t, DEVS)
        put(fsend.at[d], frecv.at[at.chip * 2 + at.core], send, recv, at.plane(d))

    times(1, DEVS, give)
    frecv[at.chip * 2 + at.core] = fsend[at.me]
    rest = frecv.at[pl.ds(0, DEVS - 1)]
    take(rest, recv)
    for b in range(2):
        for w in range(8):
            for h in range(2):
                parts = []
                for sp in range(2):
                    for q in range(2):
                        v = frecv[(2 * w + sp) * 2 + h]
                        v = v if q == b else turn(v)
                        parts.append(v if q == sp else flip(v))
                out[b, w, :, h * LANES:(h + 1) * LANES] = quadrants(*parts)
    take(rest, send)
    take(rs.at[pl.ds(0, CHIPS - 1)], rs_send)


def table_kernel(pat, order, tab, place):
    at = Place()
    for o in range(NB):
        tab[o] = jnp.int32(ROWS)
    for q in range(NB):
        place[order[q]] = jnp.int32(q)
    for a in range(ROWS):
        off = pat[a, 0]
        tab[off] = jnp.int32(a)
        tab[OFF + a] = off
        for q in range(2):
            tab[POS + q * ROWS + a] = place[(order[4 * at.r + 2 * at.core + q] + off) & (NB - 1)]


def split(v):
    hi = v.astype(BF16)
    return hi, (v - hi.astype(F32)).astype(BF16)


def dot3(a, b):
    def one(u, v):
        return jnp.dot(u, v, preferred_element_type=F32)

    return one(a[0], b[0]) + (one(a[0], b[1]) + one(a[1], b[0]))


def product_kernel(x, bbuf, tab, ct, sq, xa, ghi, glo, bm, tt, wide):
    at = Place()
    low = lane_low()
    top = row_low()
    offs = [tab[OFF + a] for a in range(ROWS)]
    for q in range(2):
        for a in range(ROWS):
            i = tab[POS + q * ROWS + a]
            ahead = (at.r - (i >> 2)) & (PLANES - 1)
            o = jnp.where(ahead == 0, 0, jnp.where(ahead <= 8, 2 * ahead - 1, 2 * (PLANES - ahead)))
            lane_keep = low if a % 2 == 0 else jnp.logical_not(low)
            even = jnp.logical_and(lane_keep, top)
            odd = jnp.logical_and(lane_keep, jnp.logical_not(top))
            for t in range(PAIRS):
                v = x[(i >> 1) & 1, o, t]
                f = flip(v)
                first = (i & 1) == 0
                e = jnp.where(first, v, f)
                d = jnp.where(first, f, v)
                for h in range(2):
                    same = h == a % 2
                    xa[q, 0, a * 10 + 2 * t + h] = jnp.where(even, e if same else turn(e), 0.0)
                    xa[q, 1, a * 10 + 2 * t + h] = jnp.where(odd, d if same else turn(d), 0.0)

    for q in range(2):
        for t in range(PAIRS):
            for w in range(8):
                u, v = bbuf[2 * w, t], bbuf[2 * w + 1, t]
                v = jnp.where(top, u, flip(v)) if q == 0 else jnp.where(top, flip(u), v)
                bm[q, 128 * t + 8 * w:128 * t + 8 * w + 8] = v[:, :64]
                bm[q, 128 * t + 64 + 8 * w:128 * t + 72 + 8 * w] = v[:, 64:]

    def rows_of(u):
        row = pl.multiple_of(16 * u, 16)
        for t in range(PAIRS):
            index = []
            for k in range(4):
                pair = [2 * t, 2 * t + 1] if 2 * t + 1 < ROWS else [2 * t]
                index.append([10 * a + tab[(4 * u + k - offs[a]) & (NB - 1)] for a in pair])
            for q in range(2):
                tiles = []
                for k in (0, 2):
                    v = xa[q, 0, index[k][0]] + xa[q, 1, index[k + 1][0]]
                    if len(index[k]) == 2:
                        v = v + (xa[q, 0, index[k][1]] + xa[q, 1, index[k + 1][1]])
                    tiles.append(v)
                hi, lo = split(jnp.concatenate(tiles, axis=0))
                ghi[q, pl.ds(row, 16), t * LANES:(t + 1) * LANES] = hi
                glo[q, pl.ds(row, 16), t * LANES:(t + 1) * LANES] = lo

    times(0, NB // 4, rows_of)
    for q in range(2):
        g = (ghi[q], glo[q])
        tmat = dot3(g, split(bm[q]))
        tt[q] = jnp.concatenate([tmat, tmat], axis=1).reshape(32, 8, LANES)
        cube = dot3(split(tmat.T), g)
        for t in range(PAIRS):
            w = cube[:, t * LANES:(t + 1) * LANES].T
            wide[q, t] = jnp.concatenate([w[:64], w[64:]], axis=1).reshape(8, 8, LANES)
    for t in range(PAIRS):
        for w in range(8):
            u, v = wide[0, t, w], wide[1, t, w]
            ct[2 * w, t] = jnp.where(top, u, flip(v))
            ct[2 * w + 1, t] = jnp.where(top, flip(u), v)
        parts = []
        for q in range(2):
            for h in range(2):
                a = 2 * t + h
                if a == ROWS:
                    parts.append(jnp.zeros((8, LANES), F32))
                    continue
                v = tt[q, offs[a] >> 1]
                parts.append(jnp.where((offs[a] & 1) == q, v, flip(v)))
        sq[t] = quadrants(*parts)


VM = pl.BlockSpec(memory_space=pltpu.VMEM)
SM = pl.BlockSpec(memory_space=pltpu.SMEM)
DMA = pltpu.SemaphoreType.DMA
SPREAD_SEMS = [DMA, DMA((PLANES,)), DMA, DMA, DMA, DMA]


def shape(*dims, dtype=F32):
    return jax.ShapeDtypeStruct(dims, dtype)


def vmem(*dims, dtype=F32):
    return pltpu.VMEM(dims, dtype)


def call(body, ident, in_specs, out_shape, scratch, out_specs=None):
    extra = {} if ident is None else {"collective_id": ident, "has_side_effects": True}
    return pl.pallas_call(
        body,
        out_shape=out_shape,
        in_specs=in_specs,
        out_specs=out_specs or jax.tree.map(lambda _: VM, out_shape),
        scratch_shapes=scratch,
        compiler_params=pltpu.CompilerParams(**extra),
    )


def local(density, pattern, grid_order):
    tab = call(
        table_kernel, None, [SM, SM], shape(TABLE, dtype=jnp.int32), [pltpu.SMEM((NB,), jnp.int32)], SM
    )(pattern.T, grid_order)
    spread_out = (shape(2, PLANES, *CHUNK), shape(CHIPS, *CHUNK))
    x, bbuf = call(
        first_kernel, 0, [VM, SM], spread_out, [vmem(NB, 8, LANES), vmem(*CHUNK), DMA, DMA] + SPREAD_SEMS
    )(density.reshape(2, 8, 8, 256), tab)
    product = call(
        product_kernel, None, [VM, VM, SM], (shape(CHIPS, *CHUNK), shape(*CHUNK)),
        [
            vmem(2, 2, ROWS * 10, 8, LANES),
            vmem(2, 4 * NB, WIDE, dtype=BF16),
            vmem(2, 4 * NB, WIDE, dtype=BF16),
            vmem(2, WIDE, 64),
            vmem(2, 32, 8, LANES),
            vmem(2, PAIRS, 8, 8, LANES),
        ],
    )
    ct, sq = product(x, bbuf, tab)
    sums = [vmem(CHIPS, *CHUNK), vmem(*CHUNK)]
    x, bbuf = call(next_kernel, 1, [VM, VM], spread_out, sums + [DMA, DMA] + SPREAD_SEMS)(ct, sq)
    ct, sq = product(x, bbuf, tab)
    out = call(
        last_kernel, 2, [VM, VM, SM, SM], shape(2, 8, 8, 256),
        sums + [vmem(10, 8, LANES), vmem(DEVS, 8, LANES), vmem(DEVS, 8, LANES), DMA, DMA, DMA, DMA],
    )(ct, sq, grid_order, tab)
    return out.reshape(128, 256)


def solution(mesh):
    in_specs = (P(("col", "rep"), "row"), P(), P())
    out_specs = P(("col", "rep"), "row")
    return jax.shard_map(local, mesh=mesh, in_specs=in_specs, out_specs=out_specs, check_vma=False)
```

time: 452 us -> 95.2 us (0.21); the launches traced: 444 us -> 94.9 us
  waiting for transfers between devices: 407 us -> 0 us
  Pallas kernels: 0 us -> 93.3 us
  matrix products: 22.4 us -> 0 us
  between operations: 13.5 us -> 0.03 us
    all_gather x6 -> x0, waiting for transfers between devices: 405 us -> none  [the longest x4 263 us: fold_product(): lax.all_gather(left, 'row', axis=1, tiled=True)]
    pallas_call x0 -> x6, Pallas kernels: none -> 93.3 us  [the longest x1 36.9 us: local(): call(first_kernel, 0, [VM, SM], spread_out, [vmem(NB, 8, LANES), vmem(*CH...]
    dot_general x4 -> x0, matrix products: 22.4 us -> none  [fold_product(): jnp.dot(lax.all_gather(left, 'row', axis=1, tiled=True), panel, precision...]
  transfers between devices with their start and end apart: 6 -> 0, of which waited for: 6 -> 0; matrix products, arithmetic and copies ran while one was open for 0% -> 0% of each run, Pallas kernels for 0% -> 0%
where the time goes in v2:
time: 95.2 us; the launch traced here: 94.9 us
  Pallas kernels  93.3 us (98%)
  local copies, waits for them, and re-layouts  1.57 us (2%)
    pallas_call x1, Pallas kernels, local(): call(first_kernel, 0, [VM, SM], spread_out, [vmem(NB, 8, LANES), vmem(*CH...  36.9 us
    pallas_call x1, Pallas kernels, local(): call(next_kernel, 1, [VM, VM], spread_out, sums + [DMA, DMA] + SPREAD_SEMS)  25.1 us
    pallas_call x1, Pallas kernels, local(): call(last_kernel, 2, [VM, VM, SM, SM], shape(2, 8, 8, 256), sums + [vmem(...  20 us
    pallas_call x2, Pallas kernels, local(): ct, sq = product(x, bbuf, tab)  9.77 us

profile of v2, /device:TPU:1, one launch (start us, length us, event | category | flops | bytes accessed | tf_op | source)
XLA Modules:
  0.0 94.9 jit_solution(7158827786879623246)
XLA Ops:
  0.0 1.5 %shard_map.37.tab = s32[96]{0:T(128)} custom-call(s32[9,64]{1,0:T(8,128)} %bitcast.5, s32[64]{0:T(128)} %order.3), custom_call_target="tpu_custom_call" | custom-call | tf_op jit(solution)/shard_map/pallas_call | solution.py:377
  1.5 36.9 %shard_map.38 = (f32[2,16,5,8,128]{4,3,2,1,0:T(8,128)}, f32[16,5,8,128]{3,2,1,0:T(8,128)}) custom-call(f32[2,8,8,256]{3,2,1,0:T(8,128)} %bitcast.4, s32[96]{0:T(128)} %shard_map.37.tab), custom_call_target="tpu_custom_call" | custom-call | tf_op jit(solution)/shard_map/pallas_call | solution.py:381
  38.4 4.9 %shard_map.39 = (f32[16,5,8,128]{3,2,1,0:T(8,128)}, f32[5,8,128]{2,1,0:T(8,128)}) custom-call(f32[2,16,5,8,128]{4,3,2,1,0:T(8,128)} %get-tuple-element.13.x, f32[16,5,8,128]{3,2,1,0:T(8,128)} %get-tuple-element.14.bbuf, s32[96]{0:T(128)} %shard_map.37.tab), custom_call_target="tpu_custom_call" | custom-call | tf_op jit(solution)/shard_map/pallas_call | solution.py:395
  43.3 25.1 %shard_map.40 = (f32[2,16,5,8,128]{4,3,2,1,0:T(8,128)}, f32[16,5,8,128]{3,2,1,0:T(8,128)}) custom-call(f32[16,5,8,128]{3,2,1,0:T(8,128)} %get-tuple-element.15.ct, f32[5,8,128]{2,1,0:T(8,128)} %get-tuple-element.16.sq), custom_call_target="tpu_custom_call" | custom-call | tf_op jit(solution)/shard_map/pallas_call | solution.py:397
  68.4 4.9 %shard_map.41 = (f32[16,5,8,128]{3,2,1,0:T(8,128)}, f32[5,8,128]{2,1,0:T(8,128)}) custom-call(f32[2,16,5,8,128]{4,3,2,1,0:T(8,128)} %get-tuple-element.17.x, f32[16,5,8,128]{3,2,1,0:T(8,128)} %get-tuple-element.18.bbuf, s32[96]{0:T(128)} %shard_map.37.tab), custom_call_target="tpu_custom_call" | custom-call | tf_op jit(solution)/shard_map/pallas_call | solution.py:398
  73.3 20.0 %shard_map.42 = f32[2,8,8,256]{3,2,1,0:T(8,128)} custom-call(f32[16,5,8,128]{3,2,1,0:T(8,128)} %get-tuple-element.19.ct, f32[5,8,128]{2,1,0:T(8,128)} %get-tuple-element.20.sq, s32[64]{0:T(128)} %order.3, s32[96]{0:T(128)} %shard_map.37.tab), custom_call_target="tpu_custom_call" | custom-call | tf_op jit(solution)/shard_map/pallas_call | solution.py:399
  93.3 1.6 %copy.5 = f32[128,256]{1,0:T(8,128)} copy(f32[128,256]{1,0:T(8,128)} %bitcast.3) | data formatting | bytes 262144

commit v3 on v2

--- a/solution.py
+++ b/solution.py
@@ -137,17 +137,9 @@
             put(part, part, sib_send, sib_recv, at.sibling)
     take(bbuf.at[pl.ds(0, CHIPS - 1)], b_recv)
     take(x.at[1 - at.core], sib_recv)
-    take(mine.at[pl.ds(0, PLANES - 1)], z_send)
-    take(mine, sib_send)
-    take(bbuf.at[pl.ds(0, CHIPS - 1)], b_send)
-
-
-def first_kernel(dens, tab, x, bbuf, landed, own, p_send, p_recv, *sems):
-    at = Place()
-    times(1, DEVS, lambda t: signal(at.plane(lax.rem(at.me + t, DEVS))))
-    greet_along(at)
-    met(DEVS - 1 + 2 * len(JUMPS))
-
+
+
+def scatter(at, dens, tab, landed, own, p_send, p_recv):
     def lanes(c):
         return pl.ds(pl.multiple_of((c % 2) * LANES, LANES), LANES)
 
@@ -159,8 +151,7 @@
 
     times(1, DEVS, one)
     landed[pl.ds(2 * at.me, 2)] = dens[:, at.chip // 2, :, lanes(at.c)]
-    rest = landed.at[pl.ds(0, 2 * (DEVS - 1))]
-    take(rest, p_recv)
+    take(landed.at[pl.ds(0, 2 * (DEVS - 1))], p_recv)
     for t in range(PAIRS):
         parts = []
         for q in range(2):
@@ -173,8 +164,6 @@
                 v = v if h == q else turn(v)
                 parts.append(jnp.where(at.p % 2 == q, v, flip(v)))
         own[t] = quadrants(*parts)
-    spread(at, own, x, bbuf, *sems)
-    take(rest, p_send)
 
 
 def reduce_slices(at, ct, sq, rs, own, send, recv):
@@ -192,22 +181,7 @@
         own[t] = 3.0 * sq[t] - 2.0 * acc
 
 
-def next_kernel(ct, sq, x, bbuf, rs, own, rs_send, rs_recv, *sems):
-    at = Place()
-    times(1, CHIPS, lambda t: signal(at.other(t)[1]))
-    signal(at.sibling)
-    greet_along(at)
-    met(CHIPS + 2 * len(JUMPS))
-    reduce_slices(at, ct, sq, rs, own, rs_send, rs_recv)
-    spread(at, own, x, bbuf, *sems)
-    take(rs.at[pl.ds(0, CHIPS - 1)], rs_send)
-
-
-def last_kernel(ct, sq, order, tab, out, rs, own, dup, fsend, frecv, rs_send, rs_recv, send, recv):
-    at = Place()
-    times(1, DEVS, lambda t: signal(at.plane(lax.rem(at.me + t, DEVS))))
-    met(DEVS - 1)
-    reduce_slices(at, ct, sq, rs, own, rs_send, rs_recv)
+def finish(at, order, tab, out, own, dup, fsend, frecv, send, recv):
     low = lane_low()
     for t in range(PAIRS):
         v = own[t]
@@ -241,8 +215,6 @@
                         v = v if q == b else turn(v)
                         parts.append(v if q == sp else flip(v))
                 out[b, w, :, h * LANES:(h + 1) * LANES] = quadrants(*parts)
-    take(rest, send)
-    take(rs.at[pl.ds(0, CHIPS - 1)], rs_send)
 
 
 def table_kernel(pat, order, tab, place):
@@ -271,8 +243,7 @@
     return one(a[0], b[0]) + (one(a[0], b[1]) + one(a[1], b[0]))
 
 
-def product_kernel(x, bbuf, tab, ct, sq, xa, ghi, glo, bm, tt, wide):
-    at = Place()
+def product(at, x, bbuf, tab, ct, sq, xa, ghi, glo, bm, tt, wide):
     low = lane_low()
     top = row_low()
     offs = [tab[OFF + a] for a in range(ROWS)]
@@ -347,59 +318,68 @@
         sq[t] = quadrants(*parts)
 
 
+def kernel(
+    dens, order, tab, out,
+    landed, own, x_a, x_b, bbuf, ct, sq, rs, xa, ghi, glo, bm, tt, wide, dup, fsend, frecv,
+    p_send, p_recv, z_send, z_recv, sib_send, sib_recv, b_send, b_recv, rs_send, rs_recv, f_send, f_recv,
+):
+    at = Place()
+    x = (x_a, x_b)
+    times(1, DEVS, lambda t: signal(at.plane(lax.rem(at.me + t, DEVS))))
+    greet_along(at)
+    met(DEVS - 1 + 2 * len(JUMPS))
+    scatter(at, dens, tab, landed, own.at[0], p_send, p_recv)
+    for k in range(2):
+        spread(
+            at, own.at[k], x[k], bbuf.at[k], z_send.at[k], z_recv.at[k], sib_send.at[k], sib_recv.at[k],
+            b_send.at[k], b_recv.at[k],
+        )
+        product(at, x[k], bbuf.at[k], tab, ct.at[k], sq, xa, ghi, glo, bm, tt, wide)
+        reduce_slices(at, ct.at[k], sq, rs.at[k], own.at[k + 1], rs_send.at[k], rs_recv.at[k])
+    finish(at, order, tab, out, own.at[2], dup, fsend, frecv, f_send, f_recv)
+    take(landed.at[pl.ds(0, 2 * (DEVS - 1))], p_send)
+    for k in range(2):
+        take(x[k].at[0, pl.ds(0, PLANES - 1)], z_send.at[k])
+        take(x[k].at[0], sib_send.at[k])
+        take(bbuf.at[k, pl.ds(0, CHIPS - 1)], b_send.at[k])
+        take(rs.at[k, pl.ds(0, CHIPS - 1)], rs_send.at[k])
+    take(frecv.at[pl.ds(0, DEVS - 1)], f_send)
+
+
 VM = pl.BlockSpec(memory_space=pltpu.VMEM)
 SM = pl.BlockSpec(memory_space=pltpu.SMEM)
 DMA = pltpu.SemaphoreType.DMA
-SPREAD_SEMS = [DMA, DMA((PLANES,)), DMA, DMA, DMA, DMA]
-
-
-def shape(*dims, dtype=F32):
-    return jax.ShapeDtypeStruct(dims, dtype)
 
 
 def vmem(*dims, dtype=F32):
     return pltpu.VMEM(dims, dtype)
 
 
-def call(body, ident, in_specs, out_shape, scratch, out_specs=None):
-    extra = {} if ident is None else {"collective_id": ident, "has_side_effects": True}
-    return pl.pallas_call(
-        body,
-        out_shape=out_shape,
-        in_specs=in_specs,
-        out_specs=out_specs or jax.tree.map(lambda _: VM, out_shape),
-        scratch_shapes=scratch,
-        compiler_params=pltpu.CompilerParams(**extra),
-    )
-
-
 def local(density, pattern, grid_order):
-    tab = call(
-        table_kernel, None, [SM, SM], shape(TABLE, dtype=jnp.int32), [pltpu.SMEM((NB,), jnp.int32)], SM
+    tab = pl.pallas_call(
+        table_kernel,
+        out_shape=jax.ShapeDtypeStruct((TABLE,), jnp.int32),
+        in_specs=[SM, SM],
+        out_specs=SM,
+        scratch_shapes=[pltpu.SMEM((NB,), jnp.int32)],
     )(pattern.T, grid_order)
-    spread_out = (shape(2, PLANES, *CHUNK), shape(CHIPS, *CHUNK))
-    x, bbuf = call(
-        first_kernel, 0, [VM, SM], spread_out, [vmem(NB, 8, LANES), vmem(*CHUNK), DMA, DMA] + SPREAD_SEMS
-    )(density.reshape(2, 8, 8, 256), tab)
-    product = call(
-        product_kernel, None, [VM, VM, SM], (shape(CHIPS, *CHUNK), shape(*CHUNK)),
-        [
-            vmem(2, 2, ROWS * 10, 8, LANES),
-            vmem(2, 4 * NB, WIDE, dtype=BF16),
-            vmem(2, 4 * NB, WIDE, dtype=BF16),
-            vmem(2, WIDE, 64),
-            vmem(2, 32, 8, LANES),
-            vmem(2, PAIRS, 8, 8, LANES),
+    out = pl.pallas_call(
+        kernel,
+        out_shape=jax.ShapeDtypeStruct((2, 8, 8, 256), F32),
+        in_specs=[VM, SM, SM],
+        out_specs=VM,
+        scratch_shapes=[
+            vmem(NB, 8, LANES), vmem(3, *CHUNK),
+            vmem(2, PLANES, *CHUNK), vmem(2, PLANES, *CHUNK), vmem(2, CHIPS, *CHUNK), vmem(2, CHIPS, *CHUNK), vmem(*CHUNK),
+            vmem(2, CHIPS, *CHUNK),
+            vmem(2, 2, ROWS * 10, 8, LANES), vmem(2, 4 * NB, WIDE, dtype=BF16), vmem(2, 4 * NB, WIDE, dtype=BF16),
+            vmem(2, WIDE, 64), vmem(2, 32, 8, LANES), vmem(2, PAIRS, 8, 8, LANES),
+            vmem(10, 8, LANES), vmem(DEVS, 8, LANES), vmem(DEVS, 8, LANES),
+            DMA, DMA, DMA((2,)), DMA((2, PLANES)), DMA((2,)), DMA((2,)), DMA((2,)), DMA((2,)), DMA((2,)), DMA((2,)),
+            DMA, DMA,
         ],
-    )
-    ct, sq = product(x, bbuf, tab)
-    sums = [vmem(CHIPS, *CHUNK), vmem(*CHUNK)]
-    x, bbuf = call(next_kernel, 1, [VM, VM], spread_out, sums + [DMA, DMA] + SPREAD_SEMS)(ct, sq)
-    ct, sq = product(x, bbuf, tab)
-    out = call(
-        last_kernel, 2, [VM, VM, SM, SM], shape(2, 8, 8, 256),
-        sums + [vmem(10, 8, LANES), vmem(DEVS, 8, LANES), vmem(DEVS, 8, LANES), DMA, DMA, DMA, DMA],
-    )(ct, sq, grid_order, tab)
+        compiler_params=pltpu.CompilerParams(collective_id=0, has_side_effects=True),
+    )(density.reshape(2, 8, 8, 256), grid_order, tab)
     return out.reshape(128, 256)
 
 

time: 95.2 us -> 80.2 us (0.84)
  Pallas kernels: 93.3 us -> 78.4 us
    pallas_call x6 -> x2, Pallas kernels: 93.3 us -> 78.4 us  [the longest x1 76.9 us: local(): pl.pallas_call(kernel, out_shape=jax.ShapeDtypeStruct((2, 8, 8, 256), F32...]
where the time goes in v3:
time: 80.2 us; the launch traced here: 80 us
  Pallas kernels  78.4 us (98%)
  local copies, waits for them, and re-layouts  1.57 us (2%)
    pallas_call x1, Pallas kernels, local(): pl.pallas_call(kernel, out_shape=jax.ShapeDtypeStruct((2, 8, 8, 256), F32...  76.9 us

profile of v3, /device:TPU:1, one launch (start us, length us, event | category | flops | bytes accessed | tf_op | source)
XLA Modules:
  0.0 80.0 jit_solution(2874796259739938993)
XLA Ops:
  0.0 1.5 %shard_map.37.tab = s32[96]{0:T(128)} custom-call(s32[9,64]{1,0:T(8,128)} %bitcast.5, s32[64]{0:T(128)} %order.3), custom_call_target="tpu_custom_call" | custom-call | tf_op jit(solution)/shard_map/pallas_call | solution.py:359
  1.5 76.9 %shard_map.38 = f32[2,8,8,256]{3,2,1,0:T(8,128)} custom-call(f32[2,8,8,256]{3,2,1,0:T(8,128)} %bitcast.4, s32[64]{0:T(128)} %order.3, s32[96]{0:T(128)} %shard_map.37.tab), custom_call_target="tpu_custom_call" | custom-call | tf_op jit(solution)/shard_map/pallas_call | solution.py:366
  78.4 1.6 %copy.5 = f32[128,256]{1,0:T(8,128)} copy(f32[128,256]{1,0:T(8,128)} %bitcast.3) | data formatting | bytes 262144

commit v4 on v3

--- a/solution.py
+++ b/solution.py
@@ -21,12 +21,15 @@
 OFF = POS + 2 * ROWS
 TABLE = 96
 
-PARENT = {1: 0, 2: 0, 4: 0, 3: 4, 5: 4, 6: 4, 7: 4, 8: 4}
+PARENT = {1: 0, 2: 0, 4: 0, 3: 4, 5: 4, 6: 4, 7: 4}
 FIRST = (4, 2, 1)
-ONWARD = (8, 7, 6, 3, 5)
-ARRIVAL = (1, 2, 4, 5, 3, 6, 7, 8)
-REACH = {1: 8, -1: 7}
-JUMPS = (1, 2, 3, 4)
+ONWARD = (7, 6, 3, 5)
+ARRIVAL = (1, 2, 4, 5, 3, 6, 7)
+JUMPS = (4, 3, 2, 1)
+SPOTS = sorted(
+    ((dx, dy) for dx in range(4) for dy in range(4) if dx or dy),
+    key=lambda o: -(min(o[0], 4 - o[0]) + min(o[1], 4 - o[1])),
+)
 
 
 class Place:
@@ -39,15 +42,22 @@
         self.chip = (self.c // 2) * 4 + self.p
         self.sibling = (self.r, self.c + 1 - 2 * self.core, self.p)
 
-    def plane(self, d):
-        return (self.r, d // 4, d % 4)
-
     def along(self, d):
         return (lax.rem(self.r + d + PLANES, PLANES), self.c, self.p)
 
-    def other(self, t):
-        d = lax.rem(self.chip + t, CHIPS)
-        return d, (self.r, (d // 4) * 2 + self.core, d % 4)
+    def spot(self, dx, dy):
+        return lax.rem(self.c // 2 + dx, 4), lax.rem(self.p + dy, 4)
+
+    def other(self, o):
+        x, y = self.spot(*o)
+        return x * 4 + y, (self.r, x * 2 + self.core, y)
+
+    def cores(self):
+        for dx, dy in SPOTS:
+            x, y = self.spot(dx, dy)
+            for h in range(2):
+                yield x, y, h, (self.r, x * 2 + h, y)
+        yield self.c // 2, self.p, 1 - self.core, self.sibling
 
 
 def put(src, dst, ssem, rsem, dev):
@@ -117,39 +127,57 @@
         for sign in (1, -1):
             send(own, sign, q)
 
-    def column(t):
-        put(own, bbuf.at[at.chip], b_send, b_recv, at.other(t)[1])
-
+    for o in SPOTS:
+        put(own, bbuf.at[at.chip], b_send, b_recv, at.other(o)[1])
     put(own, mine.at[0], sib_send, sib_recv, at.sibling)
-    times(1, CHIPS, column)
     x[at.core, 0] = own[...]
     bbuf[at.chip] = own[...]
+    side = 1 - 2 * at.core
     for q in ARRIVAL:
-        signs = [sign for sign in (1, -1) if q <= REACH[sign]]
-        for sign in signs:
+        for sign in (1, -1):
             part = mine.at[slot(sign, q)]
             take(part, z_recv.at[slot(sign, q)])
             for k in ONWARD:
-                if PARENT[k] == q and k <= REACH[sign]:
+                if PARENT[k] == q:
                     send(part, sign, k)
-        for sign in signs:
+        if q == 4:
+            put(mine.at[7 + at.core], mine.at[15], z_send, z_recv.at[15], at.along(4 * side))
+        for sign in (1, -1):
             part = mine.at[slot(sign, q)]
             put(part, part, sib_send, sib_recv, at.sibling)
+    last = mine.at[15]
+    take(last, z_recv.at[15])
+    put(last, last, sib_send, sib_recv, at.sibling)
     take(bbuf.at[pl.ds(0, CHIPS - 1)], b_recv)
     take(x.at[1 - at.core], sib_recv)
 
 
-def scatter(at, dens, tab, landed, own, p_send, p_recv):
+def fill_tables(at, pat, order, tab):
+    offs = [pat[a, 0] for a in range(ROWS)]
+    targets = [(order[4 * at.r + 2 * at.core + q] + off) & (NB - 1) for q in range(2) for off in offs]
+
+    def step(o, found):
+        v = jnp.int32(ROWS)
+        for a in range(ROWS):
+            v = jnp.where(offs[a] == o, jnp.int32(a), v)
+        tab[o] = v
+        n = order[o]
+        return tuple(jnp.where(n == target, o, f) for target, f in zip(targets, found))
+
+    found = lax.fori_loop(0, NB, step, (jnp.int32(0),) * len(targets))
+    for k, f in enumerate(found):
+        tab[POS + k] = f
+    for a in range(ROWS):
+        tab[OFF + a] = offs[a]
+
+
+def scatter(at, dens, pat, order, tab, landed, own, p_send, p_recv):
     def lanes(c):
         return pl.ds(pl.multiple_of((c % 2) * LANES, LANES), LANES)
 
-    def one(t):
-        d = lax.rem(at.me + t, DEVS)
-        dc = d // 4
-        tile_row = (dc // 2) * 2 + (d % 4) // 2
-        put(dens.at[:, tile_row, :, lanes(dc)], landed.at[pl.ds(2 * at.me, 2)], p_send, p_recv, at.plane(d))
-
-    times(1, DEVS, one)
+    for x, y, h, dev in at.cores():
+        put(dens.at[:, x * 2 + y // 2, :, lanes(h)], landed.at[pl.ds(2 * at.me, 2)], p_send, p_recv, dev)
+    fill_tables(at, pat, order, tab)
     landed[pl.ds(2 * at.me, 2)] = dens[:, at.chip // 2, :, lanes(at.c)]
     take(landed.at[pl.ds(0, 2 * (DEVS - 1))], p_recv)
     for t in range(PAIRS):
@@ -167,11 +195,9 @@
 
 
 def reduce_slices(at, ct, sq, rs, own, send, recv):
-    def one(t):
-        d, dev = at.other(t)
+    for o in SPOTS:
+        d, dev = at.other(o)
         put(ct.at[d], rs.at[at.chip], send, recv, dev)
-
-    times(1, CHIPS, one)
     rs[at.chip] = ct[at.chip]
     take(rs.at[pl.ds(0, CHIPS - 1)], recv)
     for t in range(PAIRS):
@@ -197,11 +223,8 @@
 
     times(0, DEVS, dense)
 
-    def give(t):
-        d = lax.rem(at.me + t, DEVS)
-        put(fsend.at[d], frecv.at[at.chip * 2 + at.core], send, recv, at.plane(d))
-
-    times(1, DEVS, give)
+    for x, y, h, dev in at.cores():
+        put(fsend.at[(x * 2 + h) * 4 + y], frecv.at[at.chip * 2 + at.core], send, recv, dev)
     frecv[at.chip * 2 + at.core] = fsend[at.me]
     rest = frecv.at[pl.ds(0, DEVS - 1)]
     take(rest, recv)
@@ -215,20 +238,6 @@
                         v = v if q == b else turn(v)
                         parts.append(v if q == sp else flip(v))
                 out[b, w, :, h * LANES:(h + 1) * LANES] = quadrants(*parts)
-
-
-def table_kernel(pat, order, tab, place):
-    at = Place()
-    for o in range(NB):
-        tab[o] = jnp.int32(ROWS)
-    for q in range(NB):
-        place[order[q]] = jnp.int32(q)
-    for a in range(ROWS):
-        off = pat[a, 0]
-        tab[off] = jnp.int32(a)
-        tab[OFF + a] = off
-        for q in range(2):
-            tab[POS + q * ROWS + a] = place[(order[4 * at.r + 2 * at.core + q] + off) & (NB - 1)]
 
 
 def split(v):
@@ -319,16 +328,17 @@
 
 
 def kernel(
-    dens, order, tab, out,
-    landed, own, x_a, x_b, bbuf, ct, sq, rs, xa, ghi, glo, bm, tt, wide, dup, fsend, frecv,
+    dens, pat, order, out,
+    tab, landed, own, x_a, x_b, bbuf, ct, sq, rs, xa, ghi, glo, bm, tt, wide, dup, fsend, frecv,
     p_send, p_recv, z_send, z_recv, sib_send, sib_recv, b_send, b_recv, rs_send, rs_recv, f_send, f_recv,
 ):
     at = Place()
     x = (x_a, x_b)
-    times(1, DEVS, lambda t: signal(at.plane(lax.rem(at.me + t, DEVS))))
     greet_along(at)
+    for *_, dev in at.cores():
+        signal(dev)
     met(DEVS - 1 + 2 * len(JUMPS))
-    scatter(at, dens, tab, landed, own.at[0], p_send, p_recv)
+    scatter(at, dens, pat, order, tab, landed, own.at[0], p_send, p_recv)
     for k in range(2):
         spread(
             at, own.at[k], x[k], bbuf.at[k], z_send.at[k], z_recv.at[k], sib_send.at[k], sib_recv.at[k],
@@ -356,19 +366,13 @@
 
 
 def local(density, pattern, grid_order):
-    tab = pl.pallas_call(
-        table_kernel,
-        out_shape=jax.ShapeDtypeStruct((TABLE,), jnp.int32),
-        in_specs=[SM, SM],
-        out_specs=SM,
-        scratch_shapes=[pltpu.SMEM((NB,), jnp.int32)],
-    )(pattern.T, grid_order)
     out = pl.pallas_call(
         kernel,
         out_shape=jax.ShapeDtypeStruct((2, 8, 8, 256), F32),
         in_specs=[VM, SM, SM],
         out_specs=VM,
         scratch_shapes=[
+            pltpu.SMEM((TABLE,), jnp.int32),
             vmem(NB, 8, LANES), vmem(3, *CHUNK),
             vmem(2, PLANES, *CHUNK), vmem(2, PLANES, *CHUNK), vmem(2, CHIPS, *CHUNK), vmem(2, CHIPS, *CHUNK), vmem(*CHUNK),
             vmem(2, CHIPS, *CHUNK),
@@ -378,8 +382,8 @@
             DMA, DMA, DMA((2,)), DMA((2, PLANES)), DMA((2,)), DMA((2,)), DMA((2,)), DMA((2,)), DMA((2,)), DMA((2,)),
             DMA, DMA,
         ],
-        compiler_params=pltpu.CompilerParams(collective_id=0, has_side_effects=True),
-    )(density.reshape(2, 8, 8, 256), grid_order, tab)
+        compiler_params=pltpu.CompilerParams(collective_id=0, has_side_effects=True, vmem_limit_bytes=16 << 20),
+    )(density.reshape(2, 8, 8, 256), pattern.T, grid_order)
     return out.reshape(128, 256)
 
 

time: 80.2 us -> 76.1 us (0.949)
  Pallas kernels: 78.4 us -> 73 us
  local copies, waits for them, and re-layouts: 1.57 us -> 2.91 us
    pallas_call x1, Pallas kernels: 76.9 us -> 73 us  [local(): pl.pallas_call(kernel, out_shape=jax.ShapeDtypeStruct((2, 8, 8, 256), F32...]
    pallas_call x1 -> x0, Pallas kernels: 1.45 us -> none  [local(): pl.pallas_call(table_kernel, out_shape=jax.ShapeDtypeStruct((TABLE,), jnp...]
    unnamed x1 -> x7, local copies, waits for them, and re-layouts: 1.57 us -> 2.91 us
where the time goes in v4:
time: 76.1 us; the launch traced here: 75.9 us
  Pallas kernels  73 us (96%)
  local copies, waits for them, and re-layouts  2.91 us (4%)
    pallas_call x1, Pallas kernels, local(): pl.pallas_call(kernel, out_shape=jax.ShapeDtypeStruct((2, 8, 8, 256), F32...  73 us
    unnamed x7, local copies, waits for them, and re-layouts  2.91 us

profile of v4, /device:TPU:1, one launch (start us, length us, event | category | flops | bytes accessed | tf_op | source)
XLA Modules:
  0.0 75.9 jit_solution(8059803177121946889)
XLA Ops:
  0.0 0.0 copy-start.2
  0.0 0.7 copy-done.2
  0.7 0.0 copy-start
  0.7 0.9 %copy-done = f32[128,256]{1,0:T(8,128)S(1)} copy-done((f32[128,256]{1,0:T(8,128)S(1)}, f32[128,256]{1,0:T(8,128)}, u32[]{:S(2)}) %copy-start) | copy-done | bytes 131096
  1.6 0.0 copy-start.1
  1.6 0.7 copy-done.1
  2.3 73.0 %shard_map.37 = f32[2,8,8,256]{3,2,1,0:T(8,128)S(1)} custom-call(f32[2,8,8,256]{3,2,1,0:T(8,128)S(1)} %bitcast.4, s32[9,64]{1,0:T(8,128)S(1)} %bitcast.5, s32[64]{0:T(128)S(1)} %copy-done.2), custom_call_target="tpu_custom_call" | custom-call | tf_op jit(solution)/shard_map/pallas_call | solution.py:369
  75.2 0.7 copy.5
Async XLA Ops:
  0.0 0.7 copy-start.2
  0.7 0.9 %copy-start = (f32[128,256]{1,0:T(8,128)S(1)}, f32[128,256]{1,0:T(8,128)}, u32[]{:S(2)}) copy-start(f32[128,256]{1,0:T(8,128)} %param.3) | copy-start | bytes 393220
  1.6 0.7 copy-start.1

commit v5 on v4

--- a/solution.py
+++ b/solution.py
@@ -113,7 +113,18 @@
     return jnp.where(row_low(), jnp.where(low, q00, q01), jnp.where(low, q10, q11))
 
 
-def spread(at, own, x, bbuf, z_send, z_recv, sib_send, sib_recv, b_send, b_recv):
+def block_columns(bbuf, bm):
+    top = row_low()
+    for q in range(2):
+        for t in range(PAIRS):
+            for w in range(8):
+                u, v = bbuf[2 * w, t], bbuf[2 * w + 1, t]
+                v = jnp.where(top, u, flip(v)) if q == 0 else jnp.where(top, flip(u), v)
+                bm[q, 128 * t + 8 * w:128 * t + 8 * w + 8] = v[:, :64]
+                bm[q, 128 * t + 64 + 8 * w:128 * t + 72 + 8 * w] = v[:, 64:]
+
+
+def spread(at, own, x, bbuf, bm, z_send, z_recv, sib_send, sib_recv, b_send, b_recv):
     mine = x.at[at.core]
 
     def slot(sign, q):
@@ -145,10 +156,12 @@
         for sign in (1, -1):
             part = mine.at[slot(sign, q)]
             put(part, part, sib_send, sib_recv, at.sibling)
+        if q == 4:
+            take(bbuf.at[pl.ds(0, CHIPS - 1)], b_recv)
+            block_columns(bbuf, bm)
     last = mine.at[15]
     take(last, z_recv.at[15])
     put(last, last, sib_send, sib_recv, at.sibling)
-    take(bbuf.at[pl.ds(0, CHIPS - 1)], b_recv)
     take(x.at[1 - at.core], sib_recv)
 
 
@@ -171,14 +184,19 @@
         tab[OFF + a] = offs[a]
 
 
-def scatter(at, dens, pat, order, tab, landed, own, p_send, p_recv):
+def scatter(at, dens, pat, order, tab, landed, own, tables, load, p_send, p_recv):
     def lanes(c):
         return pl.ds(pl.multiple_of((c % 2) * LANES, LANES), LANES)
 
+    own_part = pltpu.make_async_copy(
+        dens.at[:, at.chip // 2, pl.ds(4 * (at.p % 2), 4), lanes(at.c)], landed.at[pl.ds(2 * at.me, 2)], load
+    )
+    own_part.start()
     for x, y, h, dev in at.cores():
-        put(dens.at[:, x * 2 + y // 2, :, lanes(h)], landed.at[pl.ds(2 * at.me, 2)], p_send, p_recv, dev)
+        put(dens.at[:, x * 2 + y // 2, pl.ds(4 * (y % 2), 4), lanes(h)], landed.at[pl.ds(2 * at.me, 2)], p_send, p_recv, dev)
+    for copy in (*tables, own_part):
+        copy.wait()
     fill_tables(at, pat, order, tab)
-    landed[pl.ds(2 * at.me, 2)] = dens[:, at.chip // 2, :, lanes(at.c)]
     take(landed.at[pl.ds(0, 2 * (DEVS - 1))], p_recv)
     for t in range(PAIRS):
         parts = []
@@ -189,8 +207,8 @@
                     parts.append(jnp.zeros((8, LANES), F32))
                     continue
                 v = landed[tab[POS + q * ROWS + a]]
-                v = v if h == q else turn(v)
-                parts.append(jnp.where(at.p % 2 == q, v, flip(v)))
+                v = jnp.concatenate([v, v], axis=0)
+                parts.append(v if h == q else turn(v))
         own[t] = quadrants(*parts)
 
 
@@ -252,7 +270,7 @@
     return one(a[0], b[0]) + (one(a[0], b[1]) + one(a[1], b[0]))
 
 
-def product(at, x, bbuf, tab, ct, sq, xa, ghi, glo, bm, tt, wide):
+def product(at, x, tab, ct, sq, xa, ghi, glo, bm, tt, wide):
     low = lane_low()
     top = row_low()
     offs = [tab[OFF + a] for a in range(ROWS)]
@@ -274,14 +292,6 @@
                     same = h == a % 2
                     xa[q, 0, a * 10 + 2 * t + h] = jnp.where(even, e if same else turn(e), 0.0)
                     xa[q, 1, a * 10 + 2 * t + h] = jnp.where(odd, d if same else turn(d), 0.0)
-
-    for q in range(2):
-        for t in range(PAIRS):
-            for w in range(8):
-                u, v = bbuf[2 * w, t], bbuf[2 * w + 1, t]
-                v = jnp.where(top, u, flip(v)) if q == 0 else jnp.where(top, flip(u), v)
-                bm[q, 128 * t + 8 * w:128 * t + 8 * w + 8] = v[:, :64]
-                bm[q, 128 * t + 64 + 8 * w:128 * t + 72 + 8 * w] = v[:, 64:]
 
     def rows_of(u):
         row = pl.multiple_of(16 * u, 16)
@@ -328,23 +338,29 @@
 
 
 def kernel(
-    dens, pat, order, out,
-    tab, landed, own, x_a, x_b, bbuf, ct, sq, rs, xa, ghi, glo, bm, tt, wide, dup, fsend, frecv,
-    p_send, p_recv, z_send, z_recv, sib_send, sib_recv, b_send, b_recv, rs_send, rs_recv, f_send, f_recv,
+    dens, pat_hbm, order_hbm, out,
+    pat, order, tab, landed, own, x_a, x_b, bbuf, ct, sq, rs, xa, ghi, glo, bm, tt, wide, dup, fsend, frecv,
+    load, p_send, p_recv, z_send, z_recv, sib_send, sib_recv, b_send, b_recv, rs_send, rs_recv, f_send, f_recv,
 ):
     at = Place()
     x = (x_a, x_b)
+    tables = (
+        pltpu.make_async_copy(pat_hbm, pat, load.at[1]),
+        pltpu.make_async_copy(order_hbm, order, load.at[2]),
+    )
+    for copy in tables:
+        copy.start()
     greet_along(at)
     for *_, dev in at.cores():
         signal(dev)
     met(DEVS - 1 + 2 * len(JUMPS))
-    scatter(at, dens, pat, order, tab, landed, own.at[0], p_send, p_recv)
+    scatter(at, dens, pat, order, tab, landed, own.at[0], tables, load.at[0], p_send, p_recv)
     for k in range(2):
         spread(
-            at, own.at[k], x[k], bbuf.at[k], z_send.at[k], z_recv.at[k], sib_send.at[k], sib_recv.at[k],
+            at, own.at[k], x[k], bbuf.at[k], bm, z_send.at[k], z_recv.at[k], sib_send.at[k], sib_recv.at[k],
             b_send.at[k], b_recv.at[k],
         )
-        product(at, x[k], bbuf.at[k], tab, ct.at[k], sq, xa, ghi, glo, bm, tt, wide)
+        product(at, x[k], tab, ct.at[k], sq, xa, ghi, glo, bm, tt, wide)
         reduce_slices(at, ct.at[k], sq, rs.at[k], own.at[k + 1], rs_send.at[k], rs_recv.at[k])
     finish(at, order, tab, out, own.at[2], dup, fsend, frecv, f_send, f_recv)
     take(landed.at[pl.ds(0, 2 * (DEVS - 1))], p_send)
@@ -357,7 +373,7 @@
 
 
 VM = pl.BlockSpec(memory_space=pltpu.VMEM)
-SM = pl.BlockSpec(memory_space=pltpu.SMEM)
+HBM = pl.BlockSpec(memory_space=pltpu.HBM)
 DMA = pltpu.SemaphoreType.DMA
 
 
@@ -366,24 +382,25 @@
 
 
 def local(density, pattern, grid_order):
+    inputs = (density.reshape(2, 8, 8, 256), pattern.T, grid_order)
     out = pl.pallas_call(
         kernel,
         out_shape=jax.ShapeDtypeStruct((2, 8, 8, 256), F32),
-        in_specs=[VM, SM, SM],
+        in_specs=[HBM, HBM, HBM],
         out_specs=VM,
         scratch_shapes=[
-            pltpu.SMEM((TABLE,), jnp.int32),
-            vmem(NB, 8, LANES), vmem(3, *CHUNK),
+            pltpu.SMEM((ROWS, NB), jnp.int32), pltpu.SMEM((NB,), jnp.int32), pltpu.SMEM((TABLE,), jnp.int32),
+            vmem(NB, 4, LANES), vmem(3, *CHUNK),
             vmem(2, PLANES, *CHUNK), vmem(2, PLANES, *CHUNK), vmem(2, CHIPS, *CHUNK), vmem(2, CHIPS, *CHUNK), vmem(*CHUNK),
             vmem(2, CHIPS, *CHUNK),
             vmem(2, 2, ROWS * 10, 8, LANES), vmem(2, 4 * NB, WIDE, dtype=BF16), vmem(2, 4 * NB, WIDE, dtype=BF16),
             vmem(2, WIDE, 64), vmem(2, 32, 8, LANES), vmem(2, PAIRS, 8, 8, LANES),
             vmem(10, 8, LANES), vmem(DEVS, 8, LANES), vmem(DEVS, 8, LANES),
-            DMA, DMA, DMA((2,)), DMA((2, PLANES)), DMA((2,)), DMA((2,)), DMA((2,)), DMA((2,)), DMA((2,)), DMA((2,)),
+            DMA((3,)), DMA, DMA, DMA((2,)), DMA((2, PLANES)), DMA((2,)), DMA((2,)), DMA((2,)), DMA((2,)), DMA((2,)), DMA((2,)),
             DMA, DMA,
         ],
         compiler_params=pltpu.CompilerParams(collective_id=0, has_side_effects=True, vmem_limit_bytes=16 << 20),
-    )(density.reshape(2, 8, 8, 256), pattern.T, grid_order)
+    )(*(pltpu.with_memory_space_constraint(v, pltpu.HBM) for v in inputs))
     return out.reshape(128, 256)
 
 

time: 76.1 us -> 72.4 us (0.951)
  local copies, waits for them, and re-layouts: 2.91 us -> 0.66 us
  Pallas kernels: 73 us -> 71.6 us
    unnamed x7 -> x1, local copies, waits for them, and re-layouts: 2.91 us -> 0.66 us
    pallas_call x1, Pallas kernels: 73 us -> 71.6 us  [local(): pl.pallas_call(kernel, out_shape=jax.ShapeDtypeStruct((2, 8, 8, 256), F32...]
where the time goes in v5:
time: 72.4 us; the launch traced here: 72.3 us
  Pallas kernels  71.6 us (99%)
    pallas_call x1, Pallas kernels, local(): pl.pallas_call(kernel, out_shape=jax.ShapeDtypeStruct((2, 8, 8, 256), F32...  71.6 us

profile of v5, /device:TPU:1, one launch (start us, length us, event | category | flops | bytes accessed | tf_op | source)
XLA Modules:
  0.0 72.3 jit_solution(2282586780009853276)
XLA Ops:
  0.0 71.6 %shard_map.37 = f32[2,8,8,256]{3,2,1,0:T(8,128)S(1)} custom-call(f32[2,8,8,256]{3,2,1,0:T(8,128)} %bitcast.4, s32[9,64]{1,0:T(8,128)} %bitcast.5, s32[64]{0:T(128)} %order_hbm.1), custom_call_target="tpu_custom_call" | custom-call | tf_op jit(solution)/shard_map/pallas_call | solution.py:386
  71.6 0.7 copy.5

commit v6 on v5

--- a/solution.py
+++ b/solution.py
@@ -146,13 +146,13 @@
     side = 1 - 2 * at.core
     for q in ARRIVAL:
         for sign in (1, -1):
-            part = mine.at[slot(sign, q)]
-            take(part, z_recv.at[slot(sign, q)])
-            for k in ONWARD:
-                if PARENT[k] == q:
-                    send(part, sign, k)
+            take(mine.at[slot(sign, q)], z_recv.at[slot(sign, q)])
         if q == 4:
             put(mine.at[7 + at.core], mine.at[15], z_send, z_recv.at[15], at.along(4 * side))
+        for k in ONWARD:
+            if PARENT[k] == q:
+                for sign in (1, -1):
+                    send(mine.at[slot(sign, q)], sign, k)
         for sign in (1, -1):
             part = mine.at[slot(sign, q)]
             put(part, part, sib_send, sib_recv, at.sibling)
@@ -165,7 +165,7 @@
     take(x.at[1 - at.core], sib_recv)
 
 
-def fill_tables(at, pat, order, tab):
+def fill_tables(at, pat, order, tab, near, dense):
     offs = [pat[a, 0] for a in range(ROWS)]
     targets = [(order[4 * at.r + 2 * at.core + q] + off) & (NB - 1) for q in range(2) for off in offs]
 
@@ -182,9 +182,18 @@
         tab[POS + k] = f
     for a in range(ROWS):
         tab[OFF + a] = offs[a]
-
-
-def scatter(at, dens, pat, order, tab, landed, own, tables, load, p_send, p_recv):
+    natural = [order[4 * at.r + 2 * at.core + q] for q in range(2)]
+
+    def look(o):
+        for a in range(ROWS):
+            near[o * ROWS + a] = 10 * a + tab[(o - offs[a]) & (NB - 1)]
+        for q in range(2):
+            dense[q * NB + o] = tab[(order[o] - natural[q]) & (NB - 1)]
+
+    times(0, NB, look)
+
+
+def scatter(at, dens, pat, order, tab, near, dense, landed, own, tables, load, p_send, p_recv):
     def lanes(c):
         return pl.ds(pl.multiple_of((c % 2) * LANES, LANES), LANES)
 
@@ -196,7 +205,7 @@
         put(dens.at[:, x * 2 + y // 2, pl.ds(4 * (y % 2), 4), lanes(h)], landed.at[pl.ds(2 * at.me, 2)], p_send, p_recv, dev)
     for copy in (*tables, own_part):
         copy.wait()
-    fill_tables(at, pat, order, tab)
+    fill_tables(at, pat, order, tab, near, dense)
     take(landed.at[pl.ds(0, 2 * (DEVS - 1))], p_recv)
     for t in range(PAIRS):
         parts = []
@@ -225,21 +234,18 @@
         own[t] = 3.0 * sq[t] - 2.0 * acc
 
 
-def finish(at, order, tab, out, own, dup, fsend, frecv, send, recv):
+def finish(at, dense, out, own, dup, fsend, frecv, send, recv):
     low = lane_low()
     for t in range(PAIRS):
         v = own[t]
         w = turn(v)
         dup[2 * t] = jnp.where(low, v, w)
         dup[2 * t + 1] = jnp.where(low, w, v)
-    n0 = order[4 * at.r + 2 * at.core]
-    n1 = order[4 * at.r + 2 * at.core + 1]
-
-    def dense(d):
-        parts = [dup[tab[(order[2 * d + b] - n) & (NB - 1)]] for n in (n0, n1) for b in range(2)]
-        fsend[d] = quadrants(*parts)
-
-    times(0, DEVS, dense)
+
+    def rows_for(d):
+        fsend[d] = quadrants(*(dup[dense[q * NB + 2 * d + b]] for q in range(2) for b in range(2)))
+
+    times(0, DEVS, rows_for)
 
     for x, y, h, dev in at.cores():
         put(fsend.at[(x * 2 + h) * 4 + y], frecv.at[at.chip * 2 + at.core], send, recv, dev)
@@ -270,7 +276,7 @@
     return one(a[0], b[0]) + (one(a[0], b[1]) + one(a[1], b[0]))
 
 
-def product(at, x, tab, ct, sq, xa, ghi, glo, bm, tt, wide):
+def product(at, x, tab, near, ct, sq, xa, ghi, glo, bm, tt, wide):
     low = lane_low()
     top = row_low()
     offs = [tab[OFF + a] for a in range(ROWS)]
@@ -299,7 +305,7 @@
             index = []
             for k in range(4):
                 pair = [2 * t, 2 * t + 1] if 2 * t + 1 < ROWS else [2 * t]
-                index.append([10 * a + tab[(4 * u + k - offs[a]) & (NB - 1)] for a in pair])
+                index.append([near[(4 * u + k) * ROWS + a] for a in pair])
             for q in range(2):
                 tiles = []
                 for k in (0, 2):
@@ -339,7 +345,7 @@
 
 def kernel(
     dens, pat_hbm, order_hbm, out,
-    pat, order, tab, landed, own, x_a, x_b, bbuf, ct, sq, rs, xa, ghi, glo, bm, tt, wide, dup, fsend, frecv,
+    pat, order, tab, near, dense, landed, own, x_a, x_b, bbuf, ct, sq, rs, xa, ghi, glo, bm, tt, wide, dup, fsend, frecv,
     load, p_send, p_recv, z_send, z_recv, sib_send, sib_recv, b_send, b_recv, rs_send, rs_recv, f_send, f_recv,
 ):
     at = Place()
@@ -354,15 +360,15 @@
     for *_, dev in at.cores():
         signal(dev)
     met(DEVS - 1 + 2 * len(JUMPS))
-    scatter(at, dens, pat, order, tab, landed, own.at[0], tables, load.at[0], p_send, p_recv)
+    scatter(at, dens, pat, order, tab, near, dense, landed, own.at[0], tables, load.at[0], p_send, p_recv)
     for k in range(2):
         spread(
             at, own.at[k], x[k], bbuf.at[k], bm, z_send.at[k], z_recv.at[k], sib_send.at[k], sib_recv.at[k],
             b_send.at[k], b_recv.at[k],
         )
-        product(at, x[k], tab, ct.at[k], sq, xa, ghi, glo, bm, tt, wide)
+        product(at, x[k], tab, near, ct.at[k], sq, xa, ghi, glo, bm, tt, wide)
         reduce_slices(at, ct.at[k], sq, rs.at[k], own.at[k + 1], rs_send.at[k], rs_recv.at[k])
-    finish(at, order, tab, out, own.at[2], dup, fsend, frecv, f_send, f_recv)
+    finish(at, dense, out, own.at[2], dup, fsend, frecv, f_send, f_recv)
     take(landed.at[pl.ds(0, 2 * (DEVS - 1))], p_send)
     for k in range(2):
         take(x[k].at[0, pl.ds(0, PLANES - 1)], z_send.at[k])
@@ -390,6 +396,7 @@
         out_specs=VM,
         scratch_shapes=[
             pltpu.SMEM((ROWS, NB), jnp.int32), pltpu.SMEM((NB,), jnp.int32), pltpu.SMEM((TABLE,), jnp.int32),
+            pltpu.SMEM((NB * ROWS,), jnp.int32), pltpu.SMEM((2 * NB,), jnp.int32),
             vmem(NB, 4, LANES), vmem(3, *CHUNK),
             vmem(2, PLANES, *CHUNK), vmem(2, PLANES, *CHUNK), vmem(2, CHIPS, *CHUNK), vmem(2, CHIPS, *CHUNK), vmem(*CHUNK),
             vmem(2, CHIPS, *CHUNK),

time: 72.4 us -> 70.3 us (0.971)
  Pallas kernels: 71.6 us -> 69.5 us
    pallas_call x1, Pallas kernels: 71.6 us -> 69.5 us  [local(): pl.pallas_call(kernel, out_shape=jax.ShapeDtypeStruct((2, 8, 8, 256), F32...]
where the time goes in v6:
time: 70.3 us; the launch traced here: 70.2 us
  Pallas kernels  69.5 us (99%)
    pallas_call x1, Pallas kernels, local(): pl.pallas_call(kernel, out_shape=jax.ShapeDtypeStruct((2, 8, 8, 256), F32...  69.5 us

profile of v6, /device:TPU:1, one launch (start us, length us, event | category | flops | bytes accessed | tf_op | source)
XLA Modules:
  0.0 70.2 jit_solution(16511986819484677974)
XLA Ops:
  0.0 69.5 %shard_map.37 = f32[2,8,8,256]{3,2,1,0:T(8,128)S(1)} custom-call(f32[2,8,8,256]{3,2,1,0:T(8,128)} %bitcast.4, s32[9,64]{1,0:T(8,128)} %bitcast.5, s32[64]{0:T(128)} %order_hbm.1), custom_call_target="tpu_custom_call" | custom-call | tf_op jit(solution)/shard_map/pallas_call | solution.py:392
  69.5 0.7 copy.5
